TPU v7x, 32 devices: a whole 2x2x4 slice. The times are simulated.
32 devices in a mesh: dp: 4 (over z), span: 2 (over core), tensor: 4 (over y, x).
Axes of the slice: x: 2, y: 2, z: 4, core: 2. Of those that a mesh axis runs over, the one named last changes fastest.
Arguments:
- layer_input: bfloat16 [2, 16, 512, 768], P('span', 'dp', 'tensor'), may hold values from -6 to 6
- skip_tokens: bfloat16 [2, 16, 512, 768], P('span', 'dp', 'tensor'), may hold values from -6 to 6
- backbone_cotangent: bfloat16 [2, 16, 512, 768], P('span', 'dp', 'tensor'), may hold values from -6 to 6
- head_cotangent: bfloat16 [2, 16, 512, 768], P('span', 'dp', 'tensor'), may hold values from -6 to 6
- segment_lengths: int32 [2, 16, 4], P('span', 'dp'), may hold values from 1 to 174, 464 in all within a row
- pair_index: int32 [64], replicated, may hold values from 0 to 63, each once
- w_heads: bfloat16 [2, 3, 768, 768], P(None, None, None, 'tensor'), may hold values from -0.21875 to 0.21875
- heads_bias: bfloat16 [2, 2, 768], P(None, None, 'tensor'), may hold values from -1.75 to 1.75
- w_project: bfloat16 [2, 768, 768], P(None, 'tensor'), may hold values from -0.875 to 0.875
- project_bias: bfloat16 [2, 768], replicated, may hold values from -1.75 to 1.75
- norm_gain: bfloat16 [2, 2, 768], replicated, may hold values from 0.5 to 1.5
- norm_shift: bfloat16 [2, 2, 768], replicated, may hold values from -1.75 to 1.75
- w_expand: bfloat16 [2, 768, 3072], P(None, None, 'tensor'), may hold values from -0.21875 to 0.21875
- expand_bias: bfloat16 [2, 3072], P(None, 'tensor'), may hold values from -3 to 3
- w_shrink: bfloat16 [2, 3072, 768], P(None, 'tensor'), may hold values from -0.109375 to 0.109375
- shrink_bias: bfloat16 [2, 768], replicated, may hold values from -1.75 to 1.75
Outputs:
- backbone_out: bfloat16 [2, 16, 512, 768], P('span', 'dp', 'tensor')
- head_out: bfloat16 [2, 16, 512, 768], P('span', 'dp', 'tensor')
- span_loss: float32 [], replicated
- grad_input: bfloat16 [2, 16, 512, 768], P('span', 'dp', 'tensor')
- grad_skip: bfloat16 [2, 16, 512, 768], P('span', 'dp', 'tensor')
- grad_heads: float32 [2, 3, 768, 768], P(None, None, None, 'tensor')
- grad_heads_bias: float32 [2, 2, 768], P(None, None, 'tensor')
- grad_project: float32 [2, 768, 768], P(None, 'tensor')
- grad_project_bias: float32 [2, 768], replicated
- grad_gain: float32 [2, 2, 768], replicated
- grad_shift: float32 [2, 2, 768], replicated
- grad_expand: float32 [2, 768, 3072], P(None, None, 'tensor')
- grad_expand_bias: float32 [2, 3072], P(None, 'tensor')
- grad_shrink: float32 [2, 3072, 768], P(None, 'tensor')
- grad_shrink_bias: float32 [2, 768], replicated
Inputs may be any that keep to these rules, and one draw needn't show every extreme that they name: `segment_lengths`: each row holds 4 spans whose lengths add up to 464, the longest being 174; the rest of the row is padding. `pair_index`: each value occurs exactly once.
All inputs are finite; a program needn't handle non-finite values.
Results may differ from a plain program's by a relative error of at most 0.015.
The roundings to bfloat16 on the way count: a program that leaves them out, or rounds other values in their place, can miss the bound.
Values may be sent and summed in bfloat16 or wider, within the bound.
A program may use at most 192 MiB of HBM per device.

v0:
```python
import math
import jax
import jax.numpy as jnp
from jax import lax
from jax.sharding import PartitionSpec as P

HEAD_DIM = 64
EPSILON = 1e-12
LOSS_WEIGHT = 8.0
HIGHEST = lax.Precision.HIGHEST
MASKED = -1e30


def normalize(values, norm_scale, norm_offset):
    centred = values - jnp.mean(values, axis=-1, keepdims=True)
    spread = jnp.mean(centred * centred, axis=-1, keepdims=True)
    return centred * lax.rsqrt(spread + EPSILON) * norm_scale + norm_offset


def activate(values):
    return jax.nn.gelu(values, approximate=False)


def spread_rows(values):
    return lax.all_gather(values, "tensor", axis=1, tiled=True)


def collect_rows(values):
    return lax.psum_scatter(values, "tensor", scatter_dimension=1, tiled=True)


def split_heads(values):
    return values.reshape(values.shape[0], values.shape[1] // HEAD_DIM, HEAD_DIM)


def scores_of(queries, key_rows, segment):
    scores = (
        jnp.einsum("qhd,khd->hqk", queries, key_rows, preferred_element_type=jnp.float32) * 0.125
    )
    same_span = segment[:, None] == segment[None, :]
    return jnp.where(same_span[None], scores, MASKED)


def attend_forward(pieces):
    queries, key_rows, value_rows, segment = pieces
    queries = split_heads(queries)
    key_rows = split_heads(key_rows)
    value_rows = split_heads(value_rows)
    scores = scores_of(queries, key_rows, segment)
    maximum = jnp.max(scores, axis=-1, keepdims=True)
    raised = jnp.exp(scores - maximum)
    row_total = jnp.sum(raised, axis=-1, keepdims=True)
    attention = (raised / row_total).astype(jnp.bfloat16)
    mixture = jnp.einsum("hqk,khd->qhd", attention, value_rows, preferred_element_type=jnp.float32)
    mixture = mixture.reshape(mixture.shape[0], mixture.shape[1] * HEAD_DIM).astype(jnp.bfloat16)
    return (mixture, (maximum + jnp.log(row_total))[..., 0])


def attend_backward(pieces):
    queries, key_rows, value_rows, segment, upward, log_total = pieces
    local_width = queries.shape[1]
    queries = split_heads(queries)
    key_rows = split_heads(key_rows)
    value_rows = split_heads(value_rows)
    upward = split_heads(upward)
    scores = scores_of(queries, key_rows, segment)
    attention = jnp.exp(scores - log_total[..., None])
    grad_weights = jnp.einsum(
        "qhd,khd->hqk", upward, value_rows, preferred_element_type=jnp.float32
    )
    grad_scores = (
        attention * (grad_weights - jnp.sum(attention * grad_weights, axis=-1, keepdims=True))
    ).astype(jnp.bfloat16)
    grad_query = (
        jnp.einsum("hqk,khd->qhd", grad_scores, key_rows, preferred_element_type=jnp.float32)
        * 0.125
    )
    grad_key = (
        jnp.einsum("hqk,qhd->khd", grad_scores, queries, preferred_element_type=jnp.float32) * 0.125
    )
    grad_value = jnp.einsum(
        "hqk,qhd->khd", attention.astype(jnp.bfloat16), upward, preferred_element_type=jnp.float32
    )
    grad_query = grad_query.reshape(grad_query.shape[0], local_width).astype(jnp.bfloat16)
    grad_key = grad_key.reshape(grad_key.shape[0], local_width).astype(jnp.bfloat16)
    grad_value = grad_value.reshape(grad_value.shape[0], local_width).astype(jnp.bfloat16)
    return (grad_query, grad_key, grad_value)


def layer_forward(share, segment, weights):
    (
        w_heads,
        heads_bias,
        w_project,
        project_bias,
        norm_gain,
        norm_shift,
        w_expand,
        expand_bias,
        w_shrink,
        shrink_bias,
    ) = weights
    rows_in = spread_rows(share.astype(jnp.bfloat16))
    projected = jnp.einsum("std,cde->cste", rows_in, w_heads, preferred_element_type=jnp.float32)
    queries = (projected[0] + heads_bias[0]).astype(jnp.bfloat16)
    key_rows = projected[1].astype(jnp.bfloat16)
    value_rows = (projected[2] + heads_bias[1]).astype(jnp.bfloat16)
    mixture, log_total = lax.map(attend_forward, (queries, key_rows, value_rows, segment))
    first_sum = (
        share
        + collect_rows(
            jnp.einsum("ste,ed->std", mixture, w_project, preferred_element_type=jnp.float32)
        )
        + project_bias
    )
    first_norm = normalize(first_sum, norm_gain[0], norm_shift[0])
    rows_mid = spread_rows(first_norm.astype(jnp.bfloat16))
    expanded = (
        jnp.einsum("std,df->stf", rows_mid, w_expand, preferred_element_type=jnp.float32)
        + expand_bias
    )
    activated = activate(expanded).astype(jnp.bfloat16)
    second_sum = (
        first_norm
        + collect_rows(
            jnp.einsum("stf,fd->std", activated, w_shrink, preferred_element_type=jnp.float32)
        )
        + shrink_bias
    )
    stored = (
        rows_in,
        queries,
        key_rows,
        value_rows,
        mixture,
        log_total,
        first_sum,
        rows_mid,
        expanded,
        activated,
        second_sum,
    )
    return (normalize(second_sum, norm_gain[1], norm_shift[1]), stored)


def layer_backward(upward, segment, weights, stored):
    (
        w_heads,
        heads_bias,
        w_project,
        project_bias,
        norm_gain,
        norm_shift,
        w_expand,
        expand_bias,
        w_shrink,
        shrink_bias,
    ) = weights
    (
        rows_in,
        queries,
        key_rows,
        value_rows,
        mixture,
        log_total,
        first_sum,
        rows_mid,
        expanded,
        activated,
        second_sum,
    ) = stored
    ignored, pull_second = jax.vjp(
        normalize, second_sum, norm_gain[1].astype(jnp.float32), norm_shift[1].astype(jnp.float32)
    )
    grad_second, gain_second, shift_second = pull_second(upward)
    rounded = spread_rows(grad_second.astype(jnp.bfloat16))
    grad_shrink = jnp.einsum("stf,std->fd", activated, rounded, preferred_element_type=jnp.float32)
    grad_act = jnp.einsum("std,fd->stf", rounded, w_shrink, preferred_element_type=jnp.float32)
    ignored, pull_act = jax.vjp(activate, expanded)
    grad_hidden = pull_act(grad_act)[0]
    hidden_low = grad_hidden.astype(jnp.bfloat16)
    grad_expand = jnp.einsum(
        "std,stf->df", rows_mid, hidden_low, preferred_element_type=jnp.float32
    )
    grad_first = grad_second + collect_rows(
        jnp.einsum("stf,df->std", hidden_low, w_expand, preferred_element_type=jnp.float32)
    )
    ignored, pull_first = jax.vjp(
        normalize, first_sum, norm_gain[0].astype(jnp.float32), norm_shift[0].astype(jnp.float32)
    )
    grad_attend, gain_first, shift_first = pull_first(grad_first)
    rounded = spread_rows(grad_attend.astype(jnp.bfloat16))
    grad_project = jnp.einsum("ste,std->ed", mixture, rounded, preferred_element_type=jnp.float32)
    grad_mixture = jnp.einsum(
        "std,ed->ste", rounded, w_project, preferred_element_type=jnp.float32
    ).astype(jnp.bfloat16)
    grad_query, grad_key, grad_value = lax.map(
        attend_backward, (queries, key_rows, value_rows, segment, grad_mixture, log_total)
    )
    grad_heads = jnp.stack(
        [
            jnp.einsum("std,ste->de", rows_in, grad_query, preferred_element_type=jnp.float32),
            jnp.einsum("std,ste->de", rows_in, grad_key, preferred_element_type=jnp.float32),
            jnp.einsum("std,ste->de", rows_in, grad_value, preferred_element_type=jnp.float32),
        ]
    )
    grad_heads_bias = jnp.stack(
        [
            jnp.sum(grad_query.astype(jnp.float32), axis=(0, 1)),
            jnp.sum(grad_value.astype(jnp.float32), axis=(0, 1)),
        ]
    )
    back_terms = jnp.einsum(
        "ste,de->std", grad_query, w_heads[0], preferred_element_type=jnp.float32
    )
    back_terms = back_terms + jnp.einsum(
        "ste,de->std", grad_key, w_heads[1], preferred_element_type=jnp.float32
    )
    back_terms = back_terms + jnp.einsum(
        "ste,de->std", grad_value, w_heads[2], preferred_element_type=jnp.float32
    )
    grad_layer_in = grad_attend + collect_rows(back_terms)
    matrices = (
        grad_heads,
        grad_heads_bias,
        grad_project,
        grad_expand,
        jnp.sum(grad_hidden, axis=(0, 1)),
        grad_shrink,
    )
    vectors = (
        jnp.sum(grad_attend, axis=(0, 1)),
        jnp.stack([gain_first, gain_second]),
        jnp.stack([shift_first, shift_second]),
        jnp.sum(grad_second, axis=(0, 1)),
    )
    return (grad_layer_in, matrices, vectors)


def shards(
    layer_input,
    skip_tokens,
    backbone_cotangent,
    head_cotangent,
    segment_lengths,
    pair_index,
    w_heads,
    heads_bias,
    w_project,
    project_bias,
    norm_gain,
    norm_shift,
    w_expand,
    expand_bias,
    w_shrink,
    shrink_bias,
):
    stacked = (
        w_heads,
        heads_bias,
        w_project,
        project_bias,
        norm_gain,
        norm_shift,
        w_expand,
        expand_bias,
        w_shrink,
        shrink_bias,
    )
    backbone_weights = tuple((member[0] for member in stacked))
    head_weights = tuple((member[1] for member in stacked))
    lengths = segment_lengths[0]
    seq_count = lengths.shape[0]
    span_count = lengths.shape[1]
    share_rows = layer_input.shape[2]
    row_tokens = share_rows * lax.axis_size("tensor")
    starts = jnp.cumsum(lengths, axis=-1) - lengths
    row_length = jnp.sum(lengths, axis=-1)
    places = jnp.arange(row_tokens, dtype=jnp.int32)
    counted = jnp.sum((places[None, :, None] >= starts[:, None, :]).astype(jnp.int32), axis=-1) - 1
    segment = jnp.where(places[None, :] < row_length[:, None], counted, span_count)
    local_places = lax.axis_index("tensor") * share_rows + jnp.arange(share_rows, dtype=jnp.int32)
    valid_rows = (local_places[None, :] < row_length[:, None]).astype(jnp.float32)[..., None]
    picker = (starts[:, :, None] == local_places[None, None, :]).astype(jnp.float32)
    first_mark = jnp.sum(picker, axis=1)[..., None] > 0
    backbone, backbone_stored = layer_forward(
        layer_input[0].astype(jnp.float32), segment, backbone_weights
    )
    chosen = jnp.einsum("sgp,spd->sgd", picker, backbone, precision=HIGHEST)
    slot_count = seq_count * span_count
    feature_count = chosen.shape[2]
    gathered = lax.all_gather(
        chosen.reshape(slot_count, feature_count).astype(jnp.bfloat16),
        ("dp", "span", "tensor"),
        axis=0,
        tiled=True,
    )
    dp_count = lax.axis_size("dp")
    pair_count = lax.axis_size("span")
    tensor_count = lax.axis_size("tensor")
    anchor_rows = jnp.sum(
        gathered.astype(jnp.float32).reshape(
            dp_count, pair_count, tensor_count, slot_count, feature_count
        ),
        axis=2,
    )
    anchor_rows = jnp.transpose(anchor_rows, (1, 0, 2, 3)).reshape(
        pair_count, dp_count * slot_count, feature_count
    )
    head_input = jnp.where(first_mark, backbone, skip_tokens[0].astype(jnp.float32))
    head_rows, head_stored = layer_forward(head_input, segment, head_weights)
    vector_count = dp_count * slot_count
    side_index = lax.axis_index("span")
    block_start = lax.axis_index("dp") * slot_count
    columns = jnp.arange(vector_count, dtype=jnp.int32)
    root_width = math.sqrt(feature_count)
    logits = jnp.dot(anchor_rows[0], anchor_rows[1].T, precision=HIGHEST) / root_width
    target = (pair_index[:, None] == columns[None, :]).astype(jnp.float32)
    lse_rows = jax.nn.logsumexp(logits, axis=1)
    lse_columns = jax.nn.logsumexp(logits, axis=0)
    grad_logits = LOSS_WEIGHT * (
        jnp.exp(logits - lse_rows[:, None]) + jnp.exp(logits - lse_columns[None, :]) - 2.0 * target
    )
    grad_zero = jnp.dot(grad_logits, anchor_rows[1], precision=HIGHEST) / root_width
    grad_one = jnp.dot(grad_logits.T, anchor_rows[0], precision=HIGHEST) / root_width
    both_sides = jnp.stack([grad_zero, grad_one])
    grad_vectors = lax.dynamic_slice(
        lax.dynamic_index_in_dim(both_sides, side_index, 0, keepdims=False),
        (block_start, 0),
        (slot_count, feature_count),
    )
    span_loss = (jnp.sum(lse_rows) + jnp.sum(lse_columns) - 2.0 * jnp.sum(target * logits)) / (
        2 * vector_count
    )
    head_seed = head_cotangent[0].astype(jnp.float32) * valid_rows
    grad_head_in, head_matrices, head_vectors = layer_backward(
        head_seed, segment, head_weights, head_stored
    )
    grad_skip = jnp.where(first_mark, 0.0, grad_head_in)
    from_span = jnp.einsum(
        "sgp,sgd->spd",
        picker,
        grad_vectors.reshape(seq_count, span_count, feature_count),
        precision=HIGHEST,
    )
    backbone_seed = (
        backbone_cotangent[0].astype(jnp.float32) * valid_rows
        + jnp.where(first_mark, grad_head_in, 0.0)
        + from_span
    )
    grad_input, backbone_matrices, backbone_vectors = layer_backward(
        backbone_seed, segment, backbone_weights, backbone_stored
    )
    summed = lax.psum(
        (
            backbone_matrices[0],
            backbone_matrices[1],
            backbone_matrices[2],
            backbone_matrices[3],
            backbone_matrices[4],
            backbone_matrices[5],
            head_matrices[0],
            head_matrices[1],
            head_matrices[2],
            head_matrices[3],
            head_matrices[4],
            head_matrices[5],
        ),
        ("dp", "span"),
    )
    backbone_matrices = summed[:6]
    head_matrices = summed[6:]
    summed_small = lax.psum(
        (
            backbone_vectors[0],
            backbone_vectors[1],
            backbone_vectors[2],
            backbone_vectors[3],
            head_vectors[0],
            head_vectors[1],
            head_vectors[2],
            head_vectors[3],
        ),
        ("dp", "span", "tensor"),
    )
    backbone_vectors = summed_small[:4]
    head_vectors = summed_small[4:]
    return (
        (backbone * valid_rows).astype(jnp.bfloat16)[None],
        (head_rows * valid_rows).astype(jnp.bfloat16)[None],
        span_loss,
        grad_input.astype(jnp.bfloat16)[None],
        grad_skip.astype(jnp.bfloat16)[None],
        jnp.stack([backbone_matrices[0], head_matrices[0]]),
        jnp.stack([backbone_matrices[1], head_matrices[1]]),
        jnp.stack([backbone_matrices[2], head_matrices[2]]),
        jnp.stack([backbone_vectors[0], head_vectors[0]]),
        jnp.stack([backbone_vectors[1], head_vectors[1]]),
        jnp.stack([backbone_vectors[2], head_vectors[2]]),
        jnp.stack([backbone_matrices[3], head_matrices[3]]),
        jnp.stack([backbone_matrices[4], head_matrices[4]]),
        jnp.stack([backbone_matrices[5], head_matrices[5]]),
        jnp.stack([backbone_vectors[3], head_vectors[3]]),
    )


def solution(mesh):
    in_specs = (
        P("span", "dp", "tensor", None),
        P("span", "dp", "tensor", None),
        P("span", "dp", "tensor", None),
        P("span", "dp", "tensor", None),
        P("span", "dp", None),
        P(),
        P(None, None, None, "tensor"),
        P(None, None, "tensor"),
        P(None, "tensor", None),
        P(),
        P(),
        P(),
        P(None, None, "tensor"),
        P(None, "tensor"),
        P(None, "tensor", None),
        P(),
    )
    out_specs = (
        P("span", "dp", "tensor", None),
        P("span", "dp", "tensor", None),
        P(),
        P("span", "dp", "tensor", None),
        P("span", "dp", "tensor", None),
        P(None, None, None, "tensor"),
        P(None, None, "tensor"),
        P(None, "tensor", None),
        P(),
        P(),
        P(),
        P(None, None, "tensor"),
        P(None, "tensor"),
        P(None, "tensor", None),
        P(),
    )
    return jax.shard_map(shards, mesh=mesh, in_specs=in_specs, out_specs=out_specs, check_vma=False)
```

profile of v0, /device:TPU:0, one launch (start us, length us, event | category | flops | bytes accessed | tf_op | source)
XLA Modules:
  0.0 1523.2 jit_solution(11413857618912558488)
XLA Ops:
  11.2 45.2 %all-gather.24.cloned.1.call-done = bf16[1,4,512,768]{3,2,1,0:T(8,128)(2,1)} async-done(((bf16[1,4,128,768]{3,2,1,0:T(8,128)(2,1)}), bf16[1,4,512,768]{3,2,1,0:T(8,128)(2,1)}) %all-gather.24.cloned.1.call-update) | async-done | bytes 3145744 | tf_op jit(solution)/shard_map/all_gather | solution.py:25
  78.6 69.4 %reduce-scatter.9.cloned.1.call-done = f32[4,128,768]{2,1,0:T(8,128)} async-done(((f32[4,512,768]{2,1,0:T(8,128)}), f32[4,128,768]{2,1,0:T(8,128)}) %reduce-scatter.9.cloned.1.call-update) | async-done | bytes 1572880 | tf_op jit(solution)/shard_map/reduce_scatter | solution.py:29
  151.6 43.7 %all-gather.10.cloned.1.call-done = bf16[4,512,768]{2,1,0:T(8,128)(2,1)} async-done(((bf16[4,128,768]{2,1,0:T(8,128)(2,1)}), bf16[4,512,768]{2,1,0:T(8,128)(2,1)}) %all-gather.10.cloned.1.call-update) | async-done | bytes 3145744 | tf_op jit(solution)/shard_map/all_gather | solution.py:25
  201.8 15.4 %multiply_convert_fusion.3 = (bf16[4,512,768]{2,1,0:T(8,128)(2,1)S(1)}, f32[4,512,768]{2,1,0:T(8,128)}) fusion(f32[4,512,768]{2,1,0:T(8,128)S(1)} %get-tuple-element.398, f32[768]{0:T(1024)S(1)} %get-tuple-element.243, u8[512,768]{1,0:T(8,128)(4,1)S(1)} %get-tuple-element.212, u8[512,768]{1,0:T(8,128)(4,1)S(1)} %get-tuple-element.211), kind=kLoop, calls=%fused_computation.102 | loop fusion | flops 111673344 | bytes 16518144 | tf_op jit(solution)/shard_map/convert_element_type | solution.py:122
  224.1 69.4 %reduce-scatter.11.cloned.1.call-done = f32[4,128,768]{2,1,0:T(8,128)} async-done(((f32[4,512,768]{2,1,0:T(8,128)}), f32[4,128,768]{2,1,0:T(8,128)}) %reduce-scatter.11.cloned.1.call-update) | async-done | bytes 1572880 | tf_op jit(solution)/shard_map/reduce_scatter | solution.py:29
  298.6 43.7 %all-gather.12.cloned.1.call-done = bf16[4,512,768]{2,1,0:T(8,128)(2,1)} async-done(((bf16[4,128,768]{2,1,0:T(8,128)(2,1)}), bf16[4,512,768]{2,1,0:T(8,128)(2,1)}) %all-gather.12.cloned.1.call-update) | async-done | bytes 3145744 | tf_op jit(solution)/shard_map/all_gather | solution.py:25
  347.9 19.1 %while.53 = (s32[]{:T(128)}, bf16[4,512,192]{1,2,0:T(8,128)(2,1)S(1)}, f32[4,3,512]{2,1,0:T(4,128)S(1)}, bf16[4,512,192]{1,2,0:T(8,128)(2,1)}, s32[4,512]{1,0:T(...) while((s32[]{:T(128)}, bf16[4,512,192]{1,2,0:T(8,128)(2,1)S(1)}, ...), condition=%wide.region_17.18_spmd, body=%wide.region_14.17_spmd.sunk | while | flops 211122688 | bytes 12906601 | solution.py:108
  372.0 70.0 %reduce-scatter.13.cloned.1.call-done = f32[4,128,768]{2,1,0:T(8,128)} async-done(((f32[4,512,768]{2,1,0:T(8,128)}), f32[4,128,768]{2,1,0:T(8,128)}) %reduce-scatter.13.cloned.1.call-update) | async-done | bytes 1572880 | tf_op jit(solution)/shard_map/reduce_scatter | solution.py:29
  447.0 43.7 %all-gather.14.cloned.1.call-done = bf16[4,512,768]{2,1,0:T(8,128)(2,1)} async-done(((bf16[4,128,768]{2,1,0:T(8,128)(2,1)}), bf16[4,512,768]{2,1,0:T(8,128)(2,1)}) %all-gather.14.cloned.1.call-update) | async-done | bytes 3145744 | tf_op jit(solution)/shard_map/all_gather | solution.py:25
  497.2 15.4 %multiply_convert_fusion.2 = (bf16[4,512,768]{2,1,0:T(8,128)(2,1)S(1)}, f32[4,512,768]{2,1,0:T(8,128)}) fusion(f32[4,512,768]{2,1,0:T(8,128)S(1)} %get-tuple-element.399, f32[768]{0:T(1024)S(1)} %get-tuple-element.242, u8[512,768]{1,0:T(8,128)(4,1)S(1)} %get-tuple-element.210, u8[512,768]{1,0:T(8,128)(4,1)S(1)} %get-tuple-element.209), kind=kLoop, calls=%fused_computation.89 | loop fusion | flops 111673344 | bytes 16518144 | tf_op jit(solution)/shard_map/convert_element_type | solution.py:122
  518.8 70.1 %reduce-scatter.15.cloned.1.call-done = f32[4,128,768]{2,1,0:T(8,128)} async-done(((f32[4,512,768]{2,1,0:T(8,128)}), f32[4,128,768]{2,1,0:T(8,128)}) %reduce-scatter.15.cloned.1.call-update) | async-done | bytes 1572880 | tf_op jit(solution)/shard_map/reduce_scatter | solution.py:29
  594.5 43.5 %all-gather.16.cloned.1.call-done = bf16[4,512,768]{2,1,0:T(8,128)(2,1)} async-done(((bf16[4,128,768]{2,1,0:T(8,128)(2,1)}), bf16[4,512,768]{2,1,0:T(8,128)(2,1)}) %all-gather.16.cloned.1.call-update) | async-done | bytes 3145744 | tf_op jit(solution)/shard_map/all_gather | solution.py:25
  655.5 70.1 %reduce-scatter.17.cloned.1.call-done = f32[4,128,768]{2,1,0:T(8,128)} async-done(((f32[4,512,768]{2,1,0:T(8,128)}), f32[4,128,768]{2,1,0:T(8,128)}) %reduce-scatter.17.cloned.1.call-update) | async-done | bytes 1572880 | tf_op jit(solution)/shard_map/reduce_scatter | solution.py:29
  734.0 43.8 %all-gather.18.cloned.1.call-done = bf16[4,512,768]{2,1,0:T(8,128)(2,1)} async-done(((bf16[4,128,768]{2,1,0:T(8,128)(2,1)}), bf16[4,512,768]{2,1,0:T(8,128)(2,1)}) %all-gather.18.cloned.1.call-update) | async-done | bytes 3145744 | tf_op jit(solution)/shard_map/all_gather | solution.py:25
  782.8 36.0 %while.54 = (s32[]{:T(128)}, bf16[4,512,192]{1,2,0:T(8,128)(2,1)S(1)}, bf16[4,512,192]{1,2,0:T(8,128)(2,1)}, bf16[4,512,192]{1,2,0:T(8,128)(2,1)S(1)}, bf16[4,51...) while((s32[]{:T(128)}, ...), condition=%wide.region_39.40_spmd, body=%wide.region_37.39_spmd.sunk | while | flops 511146496 | bytes 28873352 | solution.py:197
  829.4 74.0 %all_gather.31 = bf16[512,768]{1,0:T(8,128)(2,1)S(1)} all-gather(bf16[16,768]{1,0:T(8,128)(2,1)S(1)} %convert_element_type.392), channel_id=1, replica_groups=mesh['dp'=4,'span'=2,'tensor'=4] {'dp','span','tensor'}, dimensions={0}, use_global_device_ids=true | all-gather | bytes 811008 | tf_op jit(solution)/shard_map/all_gather | solution.py:292
  916.6 43.7 %all-gather.20.cloned.1.call-done = bf16[4,512,768]{2,1,0:T(8,128)(2,1)} async-done(((bf16[4,128,768]{2,1,0:T(8,128)(2,1)}), bf16[4,512,768]{2,1,0:T(8,128)(2,1)}) %all-gather.20.cloned.1.call-update) | async-done | bytes 3145744 | tf_op jit(solution)/shard_map/all_gather | solution.py:25
  977.3 70.1 %reduce-scatter.21.cloned.1.call-done = f32[4,128,768]{2,1,0:T(8,128)} async-done(((f32[4,512,768]{2,1,0:T(8,128)}), f32[4,128,768]{2,1,0:T(8,128)}) %reduce-scatter.21.cloned.1.call-update) | async-done | bytes 1572880 | tf_op jit(solution)/shard_map/reduce_scatter | solution.py:29
  1080.1 16.4 %all-gather.22.cloned.1.call-done = bf16[4,512,768]{2,1,0:T(8,128)(2,1)} async-done(((bf16[4,128,768]{2,1,0:T(8,128)(2,1)}), bf16[4,512,768]{2,1,0:T(8,128)(2,1)}) %all-gather.22.cloned.1.call-update) | async-done | bytes 3145744 | tf_op jit(solution)/shard_map/all_gather | solution.py:25
  1103.3 41.8 %while.55 = (s32[]{:T(128)}, bf16[4,512,192]{1,2,0:T(8,128)(2,1)}, bf16[4,512,192]{1,2,0:T(8,128)(2,1)}, bf16[4,512,192]{1,2,0:T(8,128)(2,1)}, bf16[4,512,192]{1...) while((s32[]{:T(128)}, bf16[4,512,192]{1,2,0:T(8,128)(2,1)}, ...), condition=%wide.region_48.49_spmd, body=%wide.region_46.48_spmd.sunk | while | flops 511146496 | bytes 28873860 | solution.py:197
  1170.3 41.6 %all-reduce = (f32[1,768]{1,0:T(1,128)S(1)}, f32[1,768]{1,0:T(1,128)S(1)}, f32[1,2,768]{2,1,0:T(2,128)S(1)}, f32[1,2,768]{2,1,0:T(2,128)S(1)}, f32[1,2,768]{2,1,...) all-reduce(f32[1,768]{1,0:T(1,128)S(1)} %stack.204, ...), channel_id=1, replica_groups=mesh['dp'=4,'span'=2,'tensor'=4] {'dp','span','tensor'}, use_global_device_ids=true, to_apply=%region_63.64 | all-reduce | flops 9216 | bytes 73728 | tf_op jit(solution)/shard_map/psum | solution.py:373
  1215.8 29.2 %all-reduce.1 = (f32[1,2,192]{2,1,0:T(2,128)S(1)}, f32[1,2,192]{2,1,0:T(2,128)S(1)}, f32[1,768]{1,0:T(1,128)S(1)}, f32[1,768]{1,0:T(1,128)S(1)}) all-reduce(f32[1,2,192]{2,1,0:T(2,128)S(1)} %maximum_bitcast_fusion.7, f32[1,2,192]{2,1,0:T(2,128)S(1)} %maximum_bitcast_fusion.6, ...), channel_id=1, replica_groups=mesh['dp'=4,'span'=2,'tensor'=4] {'dp','span'}, use_global_device_ids=true, to_apply=%region_57.58 | all-reduce | flops 2304 | bytes 18432 | tf_op jit(solution)/shard_map/psum | solution.py:354
  1246.2 193.6 %all-reduce.5.cloned.1.call-done = (f32[1,3,768,192]{2,3,1,0:T(8,128)}, f32[1,3,768,192]{2,3,1,0:T(8,128)}, f32[1,192,768]{2,1,0:T(8,128)}, f32[1,192,768]{2,1,0...) async-done(((f32[1,3,768,192]{2,3,1,0:T(8,128)}, f32[1,3,768,192]{2,3,1,0:T(8,128)}, ...) | async-done | bytes 14155792 | tf_op jit(solution)/shard_map/psum | solution.py:354
  1453.0 59.9 %reduce-scatter.23.cloned.1.call-done = f32[4,128,768]{2,1,0:T(8,128)} async-done(((f32[4,512,768]{2,1,0:T(8,128)}), f32[4,128,768]{2,1,0:T(8,128)}) %reduce-scatter.23.cloned.1.call-update) | async-done | bytes 1572880 | tf_op jit(solution)/shard_map/reduce_scatter | solution.py:29
  (541 shorter events, 343.2 us)
Async XLA Ops:
  7.2 49.3 %all-gather.24.cloned.1.call-start = ((), (), s32[]{:S(2)}) async-start(), calls=%async_computation.23 | async-start | bytes 3932160 | tf_op jit(solution)/shard_map/all_gather | solution.py:25
  7.9 140.1 %reduce-scatter.9.cloned.1.call-start = ((), (), s32[]{:S(2)}) async-start(), calls=%async_computation.8 | async-start | bytes 7864320 | tf_op jit(solution)/shard_map/reduce_scatter | solution.py:29
  77.8 117.4 %all-gather.10.cloned.1.call-start = ((), (), s32[]{:S(2)}) async-start(), calls=%async_computation.9 | async-start | bytes 3932160 | tf_op jit(solution)/shard_map/all_gather | solution.py:25
  78.5 215.0 %copy-start.47 = (f32[768]{0:T(1024)}, f32[768]{0:T(1024)S(1)}, u32[]{:S(2)}) copy-start(f32[768]{0:T(1024)S(1)} %get-tuple-element.234) | copy-start | bytes 9220
  149.7 143.8 %copy-start.2 = (f32[4,128,768]{2,1,0:T(8,128)}, f32[4,128,768]{2,1,0:T(8,128)S(1)}, u32[]{:S(2)}) copy-start(f32[4,128,768]{2,1,0:T(8,128)S(1)} %get-tuple-element.357) | copy-start | bytes 4718596
  149.7 143.8 %copy-start.49 = (f32[4,128]{1,0:T(4,128)}, f32[4,128]{1,0:T(4,128)S(1)}, u32[]{:S(2)}) copy-start(f32[4,128]{1,0:T(4,128)S(1)} %broadcast_multiply_fusion.3) | copy-start | bytes 6148
  150.1 143.5 %copy-start.51 = (f32[4,128]{1,0:T(4,128)}, f32[4,128]{1,0:T(4,128)S(1)}, u32[]{:S(2)}) copy-start(f32[4,128]{1,0:T(4,128)S(1)} %fusion.160) | copy-start | bytes 6148
  151.3 142.2 %reduce-scatter.11.cloned.1.call-start = ((), (), s32[]{:S(2)}) async-start(), calls=%async_computation.10 | async-start | bytes 7864320 | tf_op jit(solution)/shard_map/reduce_scatter | solution.py:29
  223.3 119.0 %all-gather.12.cloned.1.call-start = ((), (), s32[]{:S(2)}) async-start(), calls=%async_computation.11 | async-start | bytes 3932160 | tf_op jit(solution)/shard_map/all_gather | solution.py:25
  298.4 143.6 %reduce-scatter.13.cloned.1.call-start = ((), (), s32[]{:S(2)}) async-start(), calls=%async_computation.12 | async-start | bytes 7864320 | tf_op jit(solution)/shard_map/reduce_scatter | solution.py:29
  371.9 118.9 %all-gather.14.cloned.1.call-start = ((), (), s32[]{:S(2)}) async-start(), calls=%async_computation.13 | async-start | bytes 3932160 | tf_op jit(solution)/shard_map/all_gather | solution.py:25
  446.7 142.2 %reduce-scatter.15.cloned.1.call-start = ((), (), s32[]{:S(2)}) async-start(), calls=%async_computation.14 | async-start | bytes 7864320 | tf_op jit(solution)/shard_map/reduce_scatter | solution.py:29
  518.8 119.2 %all-gather.16.cloned.1.call-start = ((), (), s32[]{:S(2)}) async-start(), calls=%async_computation.15 | async-start | bytes 3932160 | tf_op jit(solution)/shard_map/all_gather | solution.py:25
  594.0 131.7 %reduce-scatter.17.cloned.1.call-start = ((), (), s32[]{:S(2)}) async-start(), calls=%async_computation.16 | async-start | bytes 7864320 | tf_op jit(solution)/shard_map/reduce_scatter | solution.py:29
  655.4 122.3 %all-gather.18.cloned.1.call-start = ((), (), s32[]{:S(2)}) async-start(), calls=%async_computation.17 | async-start | bytes 3932160 | tf_op jit(solution)/shard_map/all_gather | solution.py:25
  733.7 177.3 %reduce-scatter.19.cloned.1.call-start = ((), (), s32[]{:S(2)}) async-start(), calls=%async_computation.18 | async-start | bytes 7864320 | tf_op jit(solution)/shard_map/reduce_scatter | solution.py:29
  828.3 75.6 %copy-start.70 = (s32[64]{0:T(128)S(1)}, s32[64]{0:T(128)}, u32[]{:S(2)}) copy-start(s32[64]{0:T(128)} %param.29) | copy-start | bytes 772
  828.4 132.0 %all-gather.20.cloned.1.call-start = ((), (), s32[]{:S(2)}) async-start(), calls=%async_computation.19 | async-start | bytes 3932160 | tf_op jit(solution)/shard_map/all_gather | solution.py:25
  828.4 82.6 %copy-start.6 = (f32[4,128,768]{2,1,0:T(8,128)S(1)}, f32[4,128,768]{2,1,0:T(8,128)}, u32[]{:S(2)}) copy-start(f32[4,128,768]{2,1,0:T(8,128)} %copy-done.5) | copy-start | bytes 4718596
  916.3 131.0 %reduce-scatter.21.cloned.1.call-start = ((), (), s32[]{:S(2)}) async-start(), calls=%async_computation.20 | async-start | bytes 7864320 | tf_op jit(solution)/shard_map/reduce_scatter | solution.py:29
  977.2 72.4 %copy-start.56 = (f32[4,128]{1,0:T(4,128)S(1)}, f32[4,128]{1,0:T(4,128)}, u32[]{:S(2)}) copy-start(f32[4,128]{1,0:T(4,128)} %copy-done.55) | copy-start | bytes 6148
  977.2 119.3 %all-gather.22.cloned.1.call-start = ((), (), s32[]{:S(2)}) async-start(), calls=%async_computation.21 | async-start | bytes 3932160 | tf_op jit(solution)/shard_map/all_gather | solution.py:25
  1052.5 387.3 %all-reduce.5.cloned.1.call-start = ((), (), s32[]{:S(2)}) async-start(), calls=%async_computation.24 | async-start | bytes 28311552 | tf_op jit(solution)/shard_map/psum | solution.py:354
  1153.5 359.3 %reduce-scatter.23.cloned.1.call-start = ((), (), s32[]{:S(2)}) async-start(), calls=%async_computation.22 | async-start | bytes 7864320 | tf_op jit(solution)/shard_map/reduce_scatter | solution.py:29
  (76 other events, 970.3 us)
Sparse Core Ops, SparseCore 0:
  9.8 46.5 all-gather.23
  78.0 70.0 reduce-scatter.8
  151.4 43.8 all-gather.9
  223.5 70.0 reduce-scatter.10
  298.5 43.8 all-gather.11
  372.0 70.0 reduce-scatter.12
  446.8 43.8 all-gather.13
  518.9 70.0 reduce-scatter.14
  594.1 43.8 all-gather.15
  655.5 70.0 reduce-scatter.16
  733.9 43.8 all-gather.17
  828.5 82.5 reduce-scatter.18
  916.5 43.8 all-gather.19
  977.3 70.0 reduce-scatter.20
  1052.6 43.8 all-gather.21
  1153.6 286.0 all-reduce.4
  1442.6 70.1 reduce-scatter.22
where the time goes:
time: 1530 us; the launch traced here: 1520 us
  waiting for transfers between devices  1000 us (65%)
  matrix products  173 us (11%)
  blocking collectives  145 us (9%)
  other arithmetic  109 us (7%)
  local copies, waits for them, and re-layouts  72 us (5%)
  between operations  18.6 us (1%)
    reduce_scatter x8, waiting for transfers between devices, collect_rows(): return lax.psum_scatter(values, 'tensor', scatter_dimension=1, tiled=True)  484 us
    all_gather x8, waiting for transfers between devices, spread_rows(): return lax.all_gather(values, 'tensor', axis=1, tiled=True)  324 us
    psum x1, waiting for transfers between devices, shards(): lax.psum((backbone_matrices[0], backbone_matrices[1], backbone_matrices[2...  194 us
    all_gather x1, blocking collectives, shards(): lax.all_gather(chosen.reshape(slot_count, feature_count).astype(jnp.bfloa...  74 us
    psum x1, blocking collectives, shards(): lax.psum((backbone_vectors[0], backbone_vectors[1], backbone_vectors[2],...  41.6 us
    dynamic_slice x64, local copies, waits for them, and re-layouts, layer_forward(): lax.map(attend_forward, (queries, key_rows, value_rows, segment))  38.4 us
    convert_element_type x2, other arithmetic, layer_forward(): activated = activate(expanded).astype(jnp.bfloat16)  30.8 us
  transfers between devices with their start and end apart: 17, of which 17 were waited for; matrix products, arithmetic and copies ran while one was open for 4% of the time, Pallas kernels for 0%

commit v1 on v0

--- a/solution.py
+++ b/solution.py
@@ -11,6 +11,27 @@
 MASKED = -1e30
 
 
+def gather_around(x, axis, dim):
+    size, place, rows = (lax.axis_size(axis), lax.axis_index(axis), x.shape[dim])
+    ahead = [(i, (i + 1) % size) for i in range(size)]
+    left = [(i, (i - 1) % size) for i in range(size)]
+    whole = jnp.zeros((*x.shape[:dim], size * rows, *x.shape[dim + 1 :]), x.dtype)
+    whole = lax.dynamic_update_slice_in_dim(whole, x, place * rows, axis=dim)
+    from_left = from_right = x
+    half = size // 2
+    for turn in range(1, half + 1):
+        from_left = lax.ppermute(from_left, axis, ahead)
+        whole = lax.dynamic_update_slice_in_dim(
+            whole, from_left, (place - turn) % size * rows, axis=dim
+        )
+        if turn < size - half:
+            from_right = lax.ppermute(from_right, axis, left)
+            whole = lax.dynamic_update_slice_in_dim(
+                whole, from_right, (place + turn) % size * rows, axis=dim
+            )
+    return whole
+
+
 def normalize(values, norm_scale, norm_offset):
     centred = values - jnp.mean(values, axis=-1, keepdims=True)
     spread = jnp.mean(centred * centred, axis=-1, keepdims=True)
@@ -22,7 +43,7 @@
 
 
 def spread_rows(values):
-    return lax.all_gather(values, "tensor", axis=1, tiled=True)
+    return gather_around(values, "tensor", 1)
 
 
 def collect_rows(values):

time: 1530 us -> 1630 us (1.065)
  waiting for transfers between devices: 1000 us -> 1090 us
  starting transfers between devices: 2.59 us -> 31.4 us
    ppermute x0 -> x24, waiting for transfers between devices: none -> 383 us  [the longest x16 262 us: gather_around(): from_left = lax.ppermute(from_left, axis, ahead)]
    all_gather x8 -> x0, waiting for transfers between devices: 324 us -> none  [spread_rows(): return lax.all_gather(values, 'tensor', axis=1, tiled=True)]
    psum x1, waiting for transfers between devices: 194 us -> 236 us  [shards(): lax.psum((backbone_matrices[0], backbone_matrices[1], backbone_matrices[2...]
    ppermute x0 -> x24, starting transfers between devices: none -> 30.5 us  [the longest x16 18.6 us: gather_around(): from_left = lax.ppermute(from_left, axis, ahead)]
    reduce_scatter x8, waiting for transfers between devices: 484 us -> 467 us  [collect_rows(): return lax.psum_scatter(values, 'tensor', scatter_dimension=1, tiled=True)]
  transfers between devices with their start and end apart: 17 -> 33, of which waited for: 17 -> 33; matrix products, arithmetic and copies ran while one was open for 4% -> 4% of each run, Pallas kernels for 0% -> 0%
where the time goes in v1:
time: 1630 us; the launch traced here: 1620 us
  waiting for transfers between devices  1090 us (67%)
  matrix products  160 us (10%)
  blocking collectives  140 us (9%)
  other arithmetic  103 us (6%)
  local copies, waits for them, and re-layouts  78.1 us (5%)
  starting transfers between devices  31.4 us (2%)
  between operations  19.1 us (1%)
    reduce_scatter x8, waiting for transfers between devices, collect_rows(): return lax.psum_scatter(values, 'tensor', scatter_dimension=1, tiled=True)  467 us
    ppermute x16, waiting for transfers between devices, gather_around(): from_left = lax.ppermute(from_left, axis, ahead)  262 us
    psum x1, waiting for transfers between devices, shards(): lax.psum((backbone_matrices[0], backbone_matrices[1], backbone_matrices[2...  236 us
    ppermute x8, waiting for transfers between devices, gather_around(): from_right = lax.ppermute(from_right, axis, left)  121 us
    all_gather x1, blocking collectives, shards(): lax.all_gather(chosen.reshape(slot_count, feature_count).astype(jnp.bfloa...  70.6 us
    psum x1, blocking collectives, shards(): lax.psum((backbone_vectors[0], backbone_vectors[1], backbone_vectors[2],...  40 us
    dynamic_slice x64, local copies, waits for them, and re-layouts, layer_forward(): lax.map(attend_forward, (queries, key_rows, value_rows, segment))  34.8 us
  transfers between devices with their start and end apart: 33, of which 33 were waited for; matrix products, arithmetic and copies ran while one was open for 4% of the time, Pallas kernels for 0%

profile of v1, /device:TPU:0, one launch (start us, length us, event | category | flops | bytes accessed | tf_op | source)
XLA Modules:
  0.0 1619.5 jit_solution(9411621736425316578)
XLA Ops:
  13.6 16.2 %collective-permute-done = bf16[4,128,768]{2,1,0:T(8,128)(2,1)S(1)} collective-permute-done((bf16[4,128,768]{2,1,0:T(8,128)(2,1)}, bf16[4,128,768]{2,1,0:T(8,128)(2,1)S(1)}, u32[]{:S(2)}, u32[]{:S(2)}) %collective-permute-start) | collective-permute-done | bytes 786464 | tf_op jit(solution)/shard_map/ppermute | solution.py:23
  82.8 70.0 %reduce-scatter.9.cloned.1.call-done = f32[4,128,768]{2,1,0:T(8,128)} async-done(((f32[4,512,768]{2,1,0:T(8,128)}), f32[4,128,768]{2,1,0:T(8,128)}) %reduce-scatter.9.cloned.1.call-update) | async-done | bytes 1572880 | tf_op jit(solution)/shard_map/reduce_scatter | solution.py:50
  158.5 18.4 %collective-permute-done.3 = bf16[4,128,768]{2,1,0:T(8,128)(2,1)S(1)} collective-permute-done((bf16[4,128,768]{2,1,0:T(8,128)(2,1)S(1)}, bf16[4,128,768]{2,1,0:T(8,128)(2,1)S(1)}, u32[]{:S(2)}, u32[]{:S(2)}) %collective-permute-start.3) | collective-permute-done | bytes 786464 | tf_op jit(solution)/shard_map/ppermute | solution.py:23
  178.0 15.7 collective-permute-done.4
  236.0 69.4 %reduce-scatter.11.cloned.1.call-done = f32[4,128,768]{2,1,0:T(8,128)} async-done(((f32[4,512,768]{2,1,0:T(8,128)}), f32[4,128,768]{2,1,0:T(8,128)}) %reduce-scatter.11.cloned.1.call-update) | async-done | bytes 1572880 | tf_op jit(solution)/shard_map/reduce_scatter | solution.py:50
  313.9 18.7 %collective-permute-done.6 = bf16[4,128,768]{2,1,0:T(8,128)(2,1)} collective-permute-done((bf16[4,128,768]{2,1,0:T(8,128)(2,1)}, bf16[4,128,768]{2,1,0:T(8,128)(2,1)}, u32[]{:S(2)}, u32[]{:S(2)}) %collective-permute-start.6) | collective-permute-done | bytes 786464 | tf_op jit(solution)/shard_map/ppermute | solution.py:23
  388.9 70.1 %reduce-scatter.13.cloned.1.call-done = f32[4,128,768]{2,1,0:T(8,128)} async-done(((f32[4,512,768]{2,1,0:T(8,128)}), f32[4,128,768]{2,1,0:T(8,128)}) %reduce-scatter.13.cloned.1.call-update) | async-done | bytes 1572880 | tf_op jit(solution)/shard_map/reduce_scatter | solution.py:50
  466.0 18.4 %collective-permute-done.9 = bf16[4,128,768]{2,1,0:T(8,128)(2,1)S(1)} collective-permute-done((bf16[4,128,768]{2,1,0:T(8,128)(2,1)S(1)}, bf16[4,128,768]{2,1,0:T(8,128)(2,1)S(1)}, u32[]{:S(2)}, u32[]{:S(2)}) %collective-permute-start.9) | collective-permute-done | bytes 786464 | tf_op jit(solution)/shard_map/ppermute | solution.py:23
  485.3 15.9 collective-permute-done.10
  542.6 70.1 %reduce-scatter.15.cloned.1.call-done = f32[4,128,768]{2,1,0:T(8,128)} async-done(((f32[4,512,768]{2,1,0:T(8,128)}), f32[4,128,768]{2,1,0:T(8,128)}) %reduce-scatter.15.cloned.1.call-update) | async-done | bytes 1572880 | tf_op jit(solution)/shard_map/reduce_scatter | solution.py:50
  620.1 18.4 %collective-permute-done.12 = bf16[4,128,768]{2,1,0:T(8,128)(2,1)S(1)} collective-permute-done((bf16[4,128,768]{2,1,0:T(8,128)(2,1)S(1)}, bf16[4,128,768]{2,1,0:T(8,128)(2,1)S(1)}, u32[]{:S(2)}, u32[]{:S(2)}) %collective-permute-start.12) | collective-permute-done | bytes 786464 | tf_op jit(solution)/shard_map/ppermute | solution.py:23
  639.2 16.1 collective-permute-done.13
  686.8 70.1 %reduce-scatter.17.cloned.1.call-done = f32[4,128,768]{2,1,0:T(8,128)} async-done(((f32[4,512,768]{2,1,0:T(8,128)}), f32[4,128,768]{2,1,0:T(8,128)}) %reduce-scatter.17.cloned.1.call-update) | async-done | bytes 1572880 | tf_op jit(solution)/shard_map/reduce_scatter | solution.py:50
  768.4 18.6 %collective-permute-done.15 = bf16[4,128,768]{2,1,0:T(8,128)(2,1)S(1)} collective-permute-done((bf16[4,128,768]{2,1,0:T(8,128)(2,1)}, bf16[4,128,768]{2,1,0:T(8,128)(2,1)S(1)}, u32[]{:S(2)}, u32[]{:S(2)}) %collective-permute-start.15) | collective-permute-done | bytes 786464 | tf_op jit(solution)/shard_map/ppermute | solution.py:23
  826.6 36.0 %while.54 = (s32[]{:T(128)}, bf16[4,512,192]{1,2,0:T(8,128)(2,1)S(1)}, bf16[4,512,192]{1,2,0:T(8,128)(2,1)}, bf16[4,512,192]{1,2,0:T(8,128)(2,1)S(1)}, bf16[4,51...) while((s32[]{:T(128)}, ...), condition=%wide.region_39.40_spmd, body=%wide.region_37.39_spmd.sunk | while | flops 511146496 | bytes 28873352 | solution.py:218
  873.8 70.6 %all_gather.3 = bf16[512,768]{1,0:T(8,128)(2,1)S(1)} all-gather(bf16[16,768]{1,0:T(8,128)(2,1)S(1)} %convert_element_type.392), channel_id=1, replica_groups=mesh['dp'=4,'span'=2,'tensor'=4] {'dp','span','tensor'}, dimensions={0}, use_global_device_ids=true | all-gather | bytes 811008 | tf_op jit(solution)/shard_map/all_gather | solution.py:313
  962.7 18.4 %collective-permute-done.18 = bf16[4,128,768]{2,1,0:T(8,128)(2,1)S(1)} collective-permute-done((bf16[4,128,768]{2,1,0:T(8,128)(2,1)S(1)}, bf16[4,128,768]{2,1,0:T(8,128)(2,1)S(1)}, u32[]{:S(2)}, u32[]{:S(2)}) %collective-permute-start.18) | collective-permute-done | bytes 786464 | tf_op jit(solution)/shard_map/ppermute | solution.py:23
  981.1 16.8 %collective-permute-done.19 = bf16[4,128,768]{2,1,0:T(8,128)(2,1)S(1)} collective-permute-done((bf16[4,128,768]{2,1,0:T(8,128)(2,1)S(1)}, bf16[4,128,768]{2,1,0:T(8,128)(2,1)S(1)}, u32[]{:S(2)}, u32[]{:S(2)}) %collective-permute-start.19) | collective-permute-done | bytes 786464 | tf_op jit(solution)/shard_map/ppermute | solution.py:28
  1046.1 49.9 %reduce-scatter.21.cloned.1.call-done = f32[4,128,768]{2,1,0:T(8,128)} async-done(((f32[4,512,768]{2,1,0:T(8,128)}), f32[4,128,768]{2,1,0:T(8,128)}) %reduce-scatter.21.cloned.1.call-update) | async-done | bytes 1572880 | tf_op jit(solution)/shard_map/reduce_scatter | solution.py:50
  1160.5 41.8 %while.55 = (s32[]{:T(128)}, bf16[4,512,192]{1,2,0:T(8,128)(2,1)}, bf16[4,512,192]{1,2,0:T(8,128)(2,1)}, bf16[4,512,192]{1,2,0:T(8,128)(2,1)}, bf16[4,512,192]{1...) while((s32[]{:T(128)}, bf16[4,512,192]{1,2,0:T(8,128)(2,1)}, ...), condition=%wide.region_48.49_spmd, body=%wide.region_46.48_spmd.sunk | while | flops 511146496 | bytes 28873860 | solution.py:218
  1226.7 29.2 %all-reduce.1 = (f32[1,2,192]{2,1,0:T(2,128)S(1)}, f32[1,2,192]{2,1,0:T(2,128)S(1)}, f32[1,768]{1,0:T(1,128)S(1)}, f32[1,768]{1,0:T(1,128)S(1)}) all-reduce(f32[1,2,192]{2,1,0:T(2,128)S(1)} %maximum_bitcast_fusion.7, f32[1,2,192]{2,1,0:T(2,128)S(1)} %maximum_bitcast_fusion.6, ...), channel_id=1, replica_groups=mesh['dp'=4,'span'=2,'tensor'=4] {'dp','span'}, use_global_device_ids=true, to_apply=%region_57.58 | all-reduce | flops 2304 | bytes 18432 | tf_op jit(solution)/shard_map/psum | solution.py:375
  1257.0 236.4 %all-reduce.5.cloned.1.call-done = (f32[1,3,768,192]{2,3,1,0:T(8,128)}, f32[1,3,768,192]{2,3,1,0:T(8,128)}, f32[1,192,768]{2,1,0:T(8,128)}, f32[1,192,768]{2,1,0...) async-done(((f32[1,3,768,192]{2,3,1,0:T(8,128)}, f32[1,3,768,192]{2,3,1,0:T(8,128)}, ...) | async-done | bytes 14155792 | tf_op jit(solution)/shard_map/psum | solution.py:375
  1506.6 60.0 %reduce-scatter.23.cloned.1.call-done = f32[4,128,768]{2,1,0:T(8,128)} async-done(((f32[4,512,768]{2,1,0:T(8,128)}), f32[4,128,768]{2,1,0:T(8,128)}) %reduce-scatter.23.cloned.1.call-update) | async-done | bytes 1572880 | tf_op jit(solution)/shard_map/reduce_scatter | solution.py:50
  1569.2 40.0 %all-reduce = (f32[1,768]{1,0:T(1,128)S(1)}, f32[1,768]{1,0:T(1,128)S(1)}, f32[1,2,768]{2,1,0:T(2,128)S(1)}, f32[1,2,768]{2,1,0:T(2,128)S(1)}, f32[1,2,768]{2,1,...) all-reduce(f32[1,768]{1,0:T(1,128)S(1)} %stack.204, ...), channel_id=1, replica_groups=mesh['dp'=4,'span'=2,'tensor'=4] {'dp','span','tensor'}, use_global_device_ids=true, to_apply=%region_63.64 | all-reduce | flops 9216 | bytes 73728 | tf_op jit(solution)/shard_map/psum | solution.py:394
  (647 shorter events, 599.2 us)
Async XLA Ops:
  7.2 145.6 %reduce-scatter.9.cloned.1.call-start = ((), (), s32[]{:S(2)}) async-start(), calls=%async_computation.8 | async-start | bytes 7864320 | tf_op jit(solution)/shard_map/reduce_scatter | solution.py:50
  10.3 36.9 %collective-permute-start.1 = (bf16[4,128,768]{2,1,0:T(8,128)(2,1)}, bf16[4,128,768]{2,1,0:T(8,128)(2,1)S(1)}, u32[]{:S(2)}, u32[]{:S(2)}) collective-permute-start(bf16[4,128,768]{2,1,0:T(8,128)(2,1)} %bitcast.501), channel_id=1, source_target_pairs={{0,3},{1,0},{2,1},{3,2},{4,7},{5,4},{6,5},{7,6},{8,11},{9,8},{10,9... | collective-permute-start | bytes 2359304 | tf_op jit(solution)/shard_map/ppermute | solution.py:28
  29.8 32.9 %collective-permute-start.2 = (bf16[4,128,768]{2,1,0:T(8,128)(2,1)S(1)}, bf16[4,128,768]{2,1,0:T(8,128)(2,1)S(1)}, u32[]{:S(2)}, u32[]{:S(2)}) collective-permute-start(bf16[4,128,768]{2,1,0:T(8,128)(2,1)S(1)} %collective-permute-done), channel_id=1, source_target_pairs={{0,1},{1,2},{2,3},{3,0},{4,5},{5,6},{6,7},{7,4},{8,9},{9,10},{10,1... | collective-permute-start | bytes 2359304 | tf_op jit(solution)/shard_map/ppermute | solution.py:23
  82.0 223.3 %reduce-scatter.11.cloned.1.call-start = ((), (), s32[]{:S(2)}) async-start(), calls=%async_computation.9 | async-start | bytes 7864320 | tf_op jit(solution)/shard_map/reduce_scatter | solution.py:50
  157.0 36.7 %collective-permute-start.4 = (bf16[4,128,768]{2,1,0:T(8,128)(2,1)S(1)}, bf16[4,128,768]{2,1,0:T(8,128)(2,1)S(1)}, u32[]{:S(2)}, u32[]{:S(2)}) collective-permute-start(bf16[4,128,768]{2,1,0:T(8,128)(2,1)S(1)} %get-tuple-element.369), channel_id=1, source_target_pairs={{0,3},{1,0},{2,1},{3,2},{4,7},{5,4},{6,5},{7,6},{8,11},{9,8},{10,9... | collective-permute-start | bytes 2359304 | tf_op jit(solution)/shard_map/ppermute | solution.py:28
  176.8 32.4 %collective-permute-start.5 = (bf16[4,128,768]{2,1,0:T(8,128)(2,1)S(1)}, bf16[4,128,768]{2,1,0:T(8,128)(2,1)S(1)}, u32[]{:S(2)}, u32[]{:S(2)}) collective-permute-start(bf16[4,128,768]{2,1,0:T(8,128)(2,1)S(1)} %collective-permute-done.3), channel_id=1, source_target_pairs={{0,1},{1,2},{2,3},{3,0},{4,5},{5,6},{6,7},{7,4},{8,9},{9,10},{10,1... | collective-permute-start | bytes 2359304 | tf_op jit(solution)/shard_map/ppermute | solution.py:23
  235.2 223.8 %reduce-scatter.13.cloned.1.call-start = ((), (), s32[]{:S(2)}) async-start(), calls=%async_computation.10 | async-start | bytes 7864320 | tf_op jit(solution)/shard_map/reduce_scatter | solution.py:50
  312.4 37.0 %collective-permute-start.7 = (bf16[4,128,768]{2,1,0:T(8,128)(2,1)}, bf16[4,128,768]{2,1,0:T(8,128)(2,1)}, u32[]{:S(2)}, u32[]{:S(2)}) collective-permute-start(bf16[4,128,768]{2,1,0:T(8,128)(2,1)} %get-tuple-element.363), channel_id=1, source_target_pairs={{0,3},{1,0},{2,1},{3,2},{4,7},{5,4},{6,5},{7,6},{8,11},{9,8},{10,9... | collective-permute-start | bytes 2359304 | tf_op jit(solution)/shard_map/ppermute | solution.py:28
  332.6 32.4 %collective-permute-start.8 = (bf16[4,128,768]{2,1,0:T(8,128)(2,1)}, bf16[4,128,768]{2,1,0:T(8,128)(2,1)}, u32[]{:S(2)}, u32[]{:S(2)}) collective-permute-start(bf16[4,128,768]{2,1,0:T(8,128)(2,1)} %collective-permute-done.6), channel_id=1, source_target_pairs={{0,1},{1,2},{2,3},{3,0},{4,5},{5,6},{6,7},{7,4},{8,9},{9,10},{10,1... | collective-permute-start | bytes 2359304 | tf_op jit(solution)/shard_map/ppermute | solution.py:23
  388.8 224.0 %reduce-scatter.15.cloned.1.call-start = ((), (), s32[]{:S(2)}) async-start(), calls=%async_computation.11 | async-start | bytes 7864320 | tf_op jit(solution)/shard_map/reduce_scatter | solution.py:50
  464.5 36.7 %collective-permute-start.10 = (bf16[4,128,768]{2,1,0:T(8,128)(2,1)S(1)}, bf16[4,128,768]{2,1,0:T(8,128)(2,1)S(1)}, u32[]{:S(2)}, u32[]{:S(2)}) collective-permute-start(bf16[4,128,768]{2,1,0:T(8,128)(2,1)S(1)} %get-tuple-element.359), channel_id=1, source_target_pairs={{0,3},{1,0},{2,1},{3,2},{4,7},{5,4},{6,5},{7,6},{8,11},{9,8},{10,9... | collective-permute-start | bytes 2359304 | tf_op jit(solution)/shard_map/ppermute | solution.py:28
  484.3 32.4 %collective-permute-start.11 = (bf16[4,128,768]{2,1,0:T(8,128)(2,1)S(1)}, bf16[4,128,768]{2,1,0:T(8,128)(2,1)S(1)}, u32[]{:S(2)}, u32[]{:S(2)}) collective-permute-start(bf16[4,128,768]{2,1,0:T(8,128)(2,1)S(1)} %collective-permute-done.9), channel_id=1, source_target_pairs={{0,1},{1,2},{2,3},{3,0},{4,5},{5,6},{6,7},{7,4},{8,9},{9,10},{10,1... | collective-permute-start | bytes 2359304 | tf_op jit(solution)/shard_map/ppermute | solution.py:23
  542.6 214.3 %reduce-scatter.17.cloned.1.call-start = ((), (), s32[]{:S(2)}) async-start(), calls=%async_computation.12 | async-start | bytes 7864320 | tf_op jit(solution)/shard_map/reduce_scatter | solution.py:50
  618.6 36.7 %collective-permute-start.13 = (bf16[4,128,768]{2,1,0:T(8,128)(2,1)S(1)}, bf16[4,128,768]{2,1,0:T(8,128)(2,1)S(1)}, u32[]{:S(2)}, u32[]{:S(2)}) collective-permute-start(bf16[4,128,768]{2,1,0:T(8,128)(2,1)S(1)} %get-tuple-element.349), channel_id=1, source_target_pairs={{0,3},{1,0},{2,1},{3,2},{4,7},{5,4},{6,5},{7,6},{8,11},{9,8},{10,9... | collective-permute-start | bytes 2359304 | tf_op jit(solution)/shard_map/ppermute | solution.py:28
  638.5 32.4 %collective-permute-start.14 = (bf16[4,128,768]{2,1,0:T(8,128)(2,1)S(1)}, bf16[4,128,768]{2,1,0:T(8,128)(2,1)S(1)}, u32[]{:S(2)}, u32[]{:S(2)}) collective-permute-start(bf16[4,128,768]{2,1,0:T(8,128)(2,1)S(1)} %collective-permute-done.12), channel_id=1, source_target_pairs={{0,1},{1,2},{2,3},{3,0},{4,5},{5,6},{6,7},{7,4},{8,9},{9,10},{10,1... | collective-permute-start | bytes 2359304 | tf_op jit(solution)/shard_map/ppermute | solution.py:23
  686.7 268.3 %reduce-scatter.19.cloned.1.call-start = ((), (), s32[]{:S(2)}) async-start(), calls=%async_computation.13 | async-start | bytes 7864320 | tf_op jit(solution)/shard_map/reduce_scatter | solution.py:50
  767.0 36.9 %collective-permute-start.16 = (bf16[4,128,768]{2,1,0:T(8,128)(2,1)}, bf16[4,128,768]{2,1,0:T(8,128)(2,1)S(1)}, u32[]{:S(2)}, u32[]{:S(2)}) collective-permute-start(bf16[4,128,768]{2,1,0:T(8,128)(2,1)} %get-tuple-element.344), channel_id=1, source_target_pairs={{0,3},{1,0},{2,1},{3,2},{4,7},{5,4},{6,5},{7,6},{8,11},{9,8},{10,9... | collective-permute-start | bytes 2359304 | tf_op jit(solution)/shard_map/ppermute | solution.py:28
  787.0 32.5 %collective-permute-start.17 = (bf16[4,128,768]{2,1,0:T(8,128)(2,1)S(1)}, bf16[4,128,768]{2,1,0:T(8,128)(2,1)}, u32[]{:S(2)}, u32[]{:S(2)}) collective-permute-start(bf16[4,128,768]{2,1,0:T(8,128)(2,1)S(1)} %collective-permute-done.15), channel_id=1, source_target_pairs={{0,1},{1,2},{2,3},{3,0},{4,5},{5,6},{6,7},{7,4},{8,9},{9,10},{10,1... | collective-permute-start | bytes 2359304 | tf_op jit(solution)/shard_map/ppermute | solution.py:23
  872.2 223.8 %reduce-scatter.21.cloned.1.call-start = ((), (), s32[]{:S(2)}) async-start(), calls=%async_computation.14 | async-start | bytes 7864320 | tf_op jit(solution)/shard_map/reduce_scatter | solution.py:50
  960.6 37.3 %collective-permute-start.19 = (bf16[4,128,768]{2,1,0:T(8,128)(2,1)S(1)}, bf16[4,128,768]{2,1,0:T(8,128)(2,1)S(1)}, u32[]{:S(2)}, u32[]{:S(2)}) collective-permute-start(bf16[4,128,768]{2,1,0:T(8,128)(2,1)S(1)} %get-tuple-element.340), channel_id=1, source_target_pairs={{0,3},{1,0},{2,1},{3,2},{4,7},{5,4},{6,5},{7,6},{8,11},{9,8},{10,9... | collective-permute-start | bytes 2359304 | tf_op jit(solution)/shard_map/ppermute | solution.py:28
  981.1 32.4 %collective-permute-start.20 = (bf16[4,128,768]{2,1,0:T(8,128)(2,1)S(1)}, bf16[4,128,768]{2,1,0:T(8,128)(2,1)S(1)}, u32[]{:S(2)}, u32[]{:S(2)}) collective-permute-start(bf16[4,128,768]{2,1,0:T(8,128)(2,1)S(1)} %collective-permute-done.18), channel_id=1, source_target_pairs={{0,1},{1,2},{2,3},{3,0},{4,5},{5,6},{6,7},{7,4},{8,9},{9,10},{10,1... | collective-permute-start | bytes 2359304 | tf_op jit(solution)/shard_map/ppermute | solution.py:23
  1025.7 467.8 %all-reduce.5.cloned.1.call-start = ((), (), s32[]{:S(2)}) async-start(), calls=%async_computation.16 | async-start | bytes 28311552 | tf_op jit(solution)/shard_map/psum | solution.py:375
  1121.5 32.4 %collective-permute-start.23 = (bf16[4,128,768]{2,1,0:T(8,128)(2,1)S(1)}, bf16[4,128,768]{2,1,0:T(8,128)(2,1)S(1)}, u32[]{:S(2)}, u32[]{:S(2)}) collective-permute-start(bf16[4,128,768]{2,1,0:T(8,128)(2,1)S(1)} %collective-permute-done.21), channel_id=1, source_target_pairs={{0,1},{1,2},{2,3},{3,0},{4,5},{5,6},{6,7},{7,4},{8,9},{9,10},{10,1... | collective-permute-start | bytes 2359304 | tf_op jit(solution)/shard_map/ppermute | solution.py:23
  1208.3 358.4 %reduce-scatter.23.cloned.1.call-start = ((), (), s32[]{:S(2)}) async-start(), calls=%async_computation.15 | async-start | bytes 7864320 | tf_op jit(solution)/shard_map/reduce_scatter | solution.py:50
  (115 other events, 2928.8 us)
Sparse Core Ops, SparseCore 0:
  82.1 70.5 reduce-scatter.8
  235.3 70.0 reduce-scatter.10
  388.9 70.0 reduce-scatter.12
  542.7 70.0 reduce-scatter.14
  686.8 70.0 reduce-scatter.16
  872.3 82.6 reduce-scatter.18
  1025.8 70.1 reduce-scatter.20
  1208.4 284.9 all-reduce.4
  1496.5 70.1 reduce-scatter.22
